TPU v7x, 256 devices: a whole 4x4x8 slice. The times are simulated.
256 devices in a mesh: particle: 16 (over y, z_hi), coeffici: 8 (over x, core), half: 2 (over z_lo).
Axes of the slice: x: 4, y: 4, z: 8 (z_hi: 4, z_lo: 2; z = z_hi * 2 + z_lo), core: 2. Of those that a mesh axis runs over, the one named last changes fastest.
Arguments:
- residuals: float32 [2, 16384, 16384], P('half', 'particle', 'coeffici'), may hold values from -6 to 6
- loadings: float32 [2, 16384, 256], P('half', 'coeffici'), may hold values from -0.046875 to 0.046875
Outputs:
- new_loadings: float32 [2, 16384, 256], P('half', ('coeffici', 'particle'))
- rayleigh: float32 [2, 256, 256], P('half')
All inputs are finite; a program needn't handle non-finite values.
Results may differ from a plain program's by a relative error of at most 0.00024.
Values sent between devices are 32-bit elements; how exact they have to be, the bound alone decides.
No kernel may reach another device: no remote copies, remote signals or barrier semaphores. Data moves between devices by JAX's collectives and lax.ppermute only.
A program may use at most 64 MiB of HBM per device.

v0:
```python
import math
import jax
import jax.numpy as jnp
from jax import lax
from jax.sharding import PartitionSpec as P


def from_partner(value, axis, distance):
    mask = 2**distance
    pairs = [(source, source ^ mask) for source in range(lax.axis_size(axis))]
    return lax.ppermute(value, axis, pairs)


def contract_rows(left, right):
    return lax.dot_general(
        left,
        right,
        (((0,), (0,)), ((), ())),
        precision=lax.Precision.HIGHEST,
        preferred_element_type=jnp.float32,
    )


def local(residuals, loadings):
    samples = residuals[0]
    loading = loadings[0]
    factor = 1.0 / math.sqrt(samples.shape[0] * lax.axis_size("particle"))
    partial_value = jnp.dot(
        samples, loading, precision=lax.Precision.HIGHEST, preferred_element_type=jnp.float32
    )
    scores = lax.psum(partial_value, "coeffici")
    share_rows = samples.shape[1] // lax.axis_size("particle")
    first_row = lax.axis_index("particle") * share_rows
    local_cov = contract_rows(samples, scores)
    covariance = lax.psum(local_cov, "particle") * factor
    partner = from_partner(covariance, "half", 0)
    shrunk = covariance * jax.nn.sigmoid(covariance * partner)
    correlation = contract_rows(loading, shrunk)
    rayleigh = lax.psum(correlation, "coeffici") * factor
    weighted = lax.dynamic_slice_in_dim(shrunk, first_row, share_rows, 0)
    return (weighted[None], rayleigh[None])


def solution(mesh):
    in_specs = (P("half", "particle", "coeffici"), P("half", "coeffici", None))
    out_specs = (P("half", ("coeffici", "particle"), None), P("half", None, None))
    return jax.shard_map(local, mesh=mesh, in_specs=in_specs, out_specs=out_specs, check_vma=False)
```

profile of v0, /device:TPU:8, one launch (start us, length us, event | category | flops | bytes accessed | tf_op | source)
XLA Modules:
  0.0 395.9 jit_solution(12921856936748713425)
XLA Ops:
  7.2 0.0 copy-start
  7.2 0.0 all-reduce.4.cloned.1.call-start
  7.2 1.5 copy-done
  8.8 9.9 %fusion.2 = f32[1024,256]{1,0:T(8,128)} fusion(f32[1,1024,2048]{2,1,0:T(8,128)} %param.2, f32[1,2048,256]{2,1,0:T(8,128)S(1)} %copy-done), kind=kOutput, calls=%fused_computation.2 | convolution fusion | flops 6442450944 | bytes 11534336 | tf_op jit(solution)/shard_map/dot_general | solution.py:28
  18.6 0.0 all-reduce.4.cloned.1.call-update
  18.7 0.0 all-reduce.6.cloned.1.call-start
  18.7 70.6 %all-reduce.4.cloned.1.call-done = f32[1024,256]{1,0:T(8,128)} async-done(((f32[1024,256]{1,0:T(8,128)}), f32[1024,256]{1,0:T(8,128)}) %all-reduce.4.cloned.1.call-update) | async-done | bytes 1048592 | tf_op jit(solution)/shard_map/psum | solution.py:31
  89.3 10.7 %fusion.4 = f32[2048,256]{0,1:T(8,128)} fusion(f32[1024,256]{1,0:T(8,128)} %all-reduce.4.cloned.1.call-done, f32[1,1024,2048]{2,1,0:T(8,128)} %param.2), kind=kOutput, calls=%fused_computation.4 | convolution fusion | flops 6442450944 | bytes 11534336 | tf_op jit(solution)/shard_map/dot_general | solution.py:15
  100.1 0.0 all-reduce.6.cloned.1.call-update
  100.1 0.0 all-reduce.8.cloned.1.call-start
  100.1 175.1 %all-reduce.6.cloned.1.call-done = f32[2048,256]{0,1:T(8,128)} async-done(((f32[2048,256]{0,1:T(8,128)}), f32[2048,256]{0,1:T(8,128)}) %all-reduce.6.cloned.1.call-update) | async-done | bytes 2097168 | tf_op jit(solution)/shard_map/psum | solution.py:35
  275.3 0.0 copy-start.2
  275.3 1.9 broadcast_multiply_fusion
  277.2 2.2 collective-permute-start
  279.3 38.0 %collective-permute-done = f32[2048,256]{0,1:T(8,128)S(1)} collective-permute-done((f32[2048,256]{0,1:T(8,128)S(1)}, f32[2048,256]{0,1:T(8,128)S(1)}, u32[]{:S(2)}, u32[]{:S(2)}) %collective-permute-start) | collective-permute-done | bytes 2097184 | tf_op jit(solution)/shard_map/ppermute | solution.py:11
  317.3 0.0 copy-done.2
  317.3 0.9 divide_multiply_fusion
  318.3 0.0 copy-start.1
  318.3 1.3 copy-done.1
  319.6 2.6 fusion.10
  322.2 0.0 all-reduce.8.cloned.1.call-update
  322.2 0.9 constant_dynamic-slice_fusion
  323.2 0.8 copy.5
  323.9 63.6 %all-reduce.8.cloned.1.call-done = f32[256,256]{0,1:T(8,128)} async-done(((f32[256,256]{0,1:T(8,128)}), f32[256,256]{0,1:T(8,128)}) %all-reduce.8.cloned.1.call-update) | async-done | bytes 262160 | tf_op jit(solution)/shard_map/psum | solution.py:39
  387.5 1.0 multiply_bitcast_fusion
  388.5 0.8 copy.6
Async XLA Ops:
  7.2 1.6 copy-start
  7.2 82.2 %all-reduce.4.cloned.1.call-start = ((), (), s32[]{:S(2)}) async-start(), calls=%async_computation | async-start | bytes 2097152 | tf_op jit(solution)/shard_map/psum | solution.py:31
  18.7 256.6 %all-reduce.6.cloned.1.call-start = ((), (), s32[]{:S(2)}) async-start(), calls=%async_computation.1 | async-start | bytes 4194304 | tf_op jit(solution)/shard_map/psum | solution.py:35
  100.1 287.4 %all-reduce.8.cloned.1.call-start = ((), (), s32[]{:S(2)}) async-start(), calls=%async_computation.2 | async-start | bytes 524288 | tf_op jit(solution)/shard_map/psum | solution.py:39
  275.3 42.1 %copy-start.2 = (f32[2048,256]{0,1:T(8,128)S(1)}, f32[2048,256]{0,1:T(8,128)}, u32[]{:S(2)}) copy-start(f32[2048,256]{0,1:T(8,128)} %all-reduce.6.cloned.1.call-done) | copy-start | bytes 6291460
  277.2 40.2 %collective-permute-start = (f32[2048,256]{0,1:T(8,128)S(1)}, f32[2048,256]{0,1:T(8,128)S(1)}, u32[]{:S(2)}, u32[]{:S(2)}) collective-permute-start(f32[2048,256]{0,1:T(8,128)S(1)} %broadcast_multiply_fusion), channel_id=1, source_target_pairs={{0,1},{1,0},{2,3},{3,2},{4,5},{5,4},{6,7},{7,6},{8,9},{9,8},{10,11... | collective-permute-start | bytes 6291464 | tf_op jit(solution)/shard_map/ppermute | solution.py:11
  318.3 1.3 copy-start.1
Sparse Core Ops, SparseCore 0:
  18.8 70.5 all-reduce.3
  100.2 175.0 all-reduce.5
  322.3 65.1 all-reduce.7
where the time goes:
time: 396 us
  waiting for transfers between devices  347 us (88%)
  matrix products  23.2 us (6%)
  between operations  13.8 us (3%)
  local copies, waits for them, and re-layouts  5.38 us (1%)
    psum x1, waiting for transfers between devices, local(): covariance = lax.psum(local_cov, 'particle') * factor  175 us
    psum x1, waiting for transfers between devices, local(): scores = lax.psum(partial_value, 'coeffici')  70.6 us
    psum x1, waiting for transfers between devices, local(): rayleigh = lax.psum(correlation, 'coeffici') * factor  63.6 us
    ppermute x1, waiting for transfers between devices, from_partner(): return lax.ppermute(value, axis, pairs)  38 us
    dot_general x2, matrix products, contract_rows(): lax.dot_general(left, right, (((0,), (0,)), ((), ())), precision=lax.Prec...  13.3 us
    dot_general x1, matrix products, local(): jnp.dot(samples, loading, precision=lax.Precision.HIGHEST, preferred_elem...  9.87 us
  transfers between devices with their start and end apart: 4, of which 4 were waited for; matrix products, arithmetic and copies ran while one was open for 0% of the time, Pallas kernels for 0%

commit v1 on v0

--- a/solution.py
+++ b/solution.py
@@ -32,7 +32,8 @@
     share_rows = samples.shape[1] // lax.axis_size("particle")
     first_row = lax.axis_index("particle") * share_rows
     local_cov = contract_rows(samples, scores)
-    covariance = lax.psum(local_cov, "particle") * factor
+    pack_the_ports = lambda inp: jnp.sum(lax.all_gather(inp, "particle"), 0)
+    covariance = pack_the_ports(local_cov) * factor
     partner = from_partner(covariance, "half", 0)
     shrunk = covariance * jax.nn.sigmoid(covariance * partner)
     correlation = contract_rows(loading, shrunk)

time: 396 us -> 635 us (1.60)
  waiting for transfers between devices: 347 us -> 553 us
  local copies, waits for them, and re-layouts: 5.38 us -> 34.1 us
  other arithmetic: 3.78 us -> 10.2 us
    all_gather x0 -> x1, waiting for transfers between devices: none -> 373 us  [local(): pack_the_ports = lambda inp: jnp.sum(lax.all_gather(inp, 'particle'), 0)]
    psum x1 -> x0, waiting for transfers between devices: 175 us -> none  [local(): covariance = lax.psum(local_cov, 'particle') * factor]
    unnamed x7 -> x6, local copies, waits for them, and re-layouts: 3.7 us -> 32.5 us
    ppermute x1, waiting for transfers between devices: 38 us -> 47.2 us  [from_partner(): return lax.ppermute(value, axis, pairs)]
    reduce_sum x0 -> x1, other arithmetic: none -> 8.14 us  [local(): pack_the_ports = lambda inp: jnp.sum(lax.all_gather(inp, 'particle'), 0)]
where the time goes in v1:
time: 635 us
  waiting for transfers between devices  553 us (87%)
  local copies, waits for them, and re-layouts  34.1 us (5%)
  matrix products  23.2 us (4%)
  between operations  13.8 us (2%)
  other arithmetic  10.2 us (2%)
    all_gather x1, waiting for transfers between devices, local(): pack_the_ports = lambda inp: jnp.sum(lax.all_gather(inp, 'particle'), 0)  373 us
    psum x1, waiting for transfers between devices, local(): scores = lax.psum(partial_value, 'coeffici')  70.7 us
    psum x1, waiting for transfers between devices, local(): rayleigh = lax.psum(correlation, 'coeffici') * factor  62.2 us
    ppermute x1, waiting for transfers between devices, from_partner(): return lax.ppermute(value, axis, pairs)  47.2 us
    unnamed x6, local copies, waits for them, and re-layouts  32.5 us
    dot_general x2, matrix products, contract_rows(): lax.dot_general(left, right, (((0,), (0,)), ((), ())), precision=lax.Prec...  13.3 us
  transfers between devices with their start and end apart: 4, of which 4 were waited for; matrix products, arithmetic and copies ran while one was open for 0% of the time, Pallas kernels for 0%

profile of v1, /device:TPU:8, one launch (start us, length us, event | category | flops | bytes accessed | tf_op | source)
XLA Modules:
  0.0 634.6 jit_solution(10022962787195907429)
XLA Ops:
  7.2 0.0 copy-start
  7.2 0.0 all-reduce.3.cloned.1.call-start
  7.2 1.5 copy-done
  8.8 9.9 %fusion.2 = f32[1024,256]{1,0:T(8,128)} fusion(f32[1,1024,2048]{2,1,0:T(8,128)} %param.2, f32[1,2048,256]{2,1,0:T(8,128)S(1)} %copy-done), kind=kOutput, calls=%fused_computation.3 | convolution fusion | flops 6442450944 | bytes 11534336 | tf_op jit(solution)/shard_map/dot_general | solution.py:28
  18.6 0.0 all-reduce.3.cloned.1.call-update
  18.7 0.0 all-gather.3.cloned.1.call-start
  18.7 70.7 %all-reduce.3.cloned.1.call-done = f32[1024,256]{1,0:T(8,128)} async-done(((f32[1024,256]{1,0:T(8,128)}), f32[1024,256]{1,0:T(8,128)}) %all-reduce.3.cloned.1.call-update) | async-done | bytes 1048592 | tf_op jit(solution)/shard_map/psum | solution.py:31
  89.4 10.7 %fusion.4 = f32[2048,256]{0,1:T(8,128)} fusion(f32[1024,256]{1,0:T(8,128)} %all-reduce.3.cloned.1.call-done, f32[1,1024,2048]{2,1,0:T(8,128)} %param.2), kind=kOutput, calls=%fused_computation.5 | convolution fusion | flops 6442450944 | bytes 11534336 | tf_op jit(solution)/shard_map/dot_general | solution.py:15
  100.1 0.0 all-gather.3.cloned.1.call-update
  100.2 0.2 all-reduce.5.cloned.1.call-start
  100.4 372.7 %all-gather.3.cloned.1.call-done = f32[32768,256]{0,1:T(8,128)} async-done(((f32[2048,256]{0,1:T(8,128)}), f32[32768,256]{0,1:T(8,128)}) %all-gather.3.cloned.1.call-update) | async-done | bytes 33554448 | tf_op jit(solution)/shard_map/all_gather | solution.py:35
  473.1 28.8 %copy.8 = f32[32,8,16,2048]{3,2,1,0:T(8,128)S(1)} copy(f32[32,8,16,2048]{3,1,2,0:T(8,128)} %bitcast.28) | data formatting | bytes 67108864
  501.9 8.1 %bitcast_reduce_fusion = f32[2048,256]{0,1:T(8,128)S(1)} fusion(f32[32,8,16,2048]{3,2,1,0:T(8,128)S(1)} %copy.8), kind=kLoop, calls=%fused_computation | loop fusion | flops 7864320 | bytes 35651584 | tf_op jit(solution)/shard_map/reduce_sum | solution.py:35
  510.0 0.2 broadcast_multiply_fusion
  510.2 0.1 collective-permute-start
  510.3 47.2 %collective-permute-done = f32[2048,256]{0,1:T(8,128)S(1)} collective-permute-done((f32[2048,256]{0,1:T(8,128)S(1)}, f32[2048,256]{0,1:T(8,128)S(1)}, u32[]{:S(2)}, u32[]{:S(2)}) %collective-permute-start) | collective-permute-done | bytes 2097184 | tf_op jit(solution)/shard_map/ppermute | solution.py:11
  557.5 0.9 divide_multiply_fusion
  558.4 0.0 copy-start.1
  558.4 1.3 copy-done.1
  559.7 2.6 fusion.10
  562.4 0.0 all-reduce.5.cloned.1.call-update
  562.4 0.9 constant_dynamic-slice_fusion
  563.3 0.8 copy.6
  564.1 62.2 %all-reduce.5.cloned.1.call-done = f32[256,256]{0,1:T(8,128)} async-done(((f32[256,256]{0,1:T(8,128)}), f32[256,256]{0,1:T(8,128)}) %all-reduce.5.cloned.1.call-update) | async-done | bytes 262160 | tf_op jit(solution)/shard_map/psum | solution.py:40
  626.3 1.0 multiply_bitcast_fusion
  627.3 0.8 copy.7
Async XLA Ops:
  7.2 1.6 copy-start
  7.2 82.3 %all-reduce.3.cloned.1.call-start = ((), (), s32[]{:S(2)}) async-start(), calls=%async_computation | async-start | bytes 2097152 | tf_op jit(solution)/shard_map/psum | solution.py:31
  18.7 454.5 %all-gather.3.cloned.1.call-start = ((), (), s32[]{:S(2)}) async-start(), calls=%async_computation.2 | async-start | bytes 35651584 | tf_op jit(solution)/shard_map/all_gather | solution.py:35
  100.2 526.1 %all-reduce.5.cloned.1.call-start = ((), (), s32[]{:S(2)}) async-start(), calls=%async_computation.1 | async-start | bytes 524288 | tf_op jit(solution)/shard_map/psum | solution.py:40
  510.2 47.3 %collective-permute-start = (f32[2048,256]{0,1:T(8,128)S(1)}, f32[2048,256]{0,1:T(8,128)S(1)}, u32[]{:S(2)}, u32[]{:S(2)}) collective-permute-start(f32[2048,256]{0,1:T(8,128)S(1)} %broadcast_multiply_fusion), channel_id=1, source_target_pairs={{0,1},{1,0},{2,3},{3,2},{4,5},{5,4},{6,7},{7,6},{8,9},{9,8},{10,11... | collective-permute-start | bytes 6291464 | tf_op jit(solution)/shard_map/ppermute | solution.py:11
  558.4 1.3 copy-start.1
Sparse Core Ops, SparseCore 0:
  18.8 70.6 all-reduce.2
  100.3 372.7 all-gather.2
  562.5 63.7 all-reduce.4
